TPU v7x, 32 devices: a whole 2x2x4 slice. The times are simulated.
32 devices in a mesh: dp: 8 (over y, x, core), tensor: 4 (over z).
Axes of the slice: x: 2, y: 2, z: 4, core: 2. Of those that a mesh axis runs over, the one named last changes fastest.
Arguments:
- tokens: bfloat16 [8192, 2048], P('dp'), may hold values from -6 to 6
- cotangent: bfloat16 [8192, 2048], P('dp'), may hold values from -6 to 6
- segment_ids: int32 [8, 1024], P('dp'), may hold values from 0 to 2, never falling along the last dimension, each value on 1 to 768 neighbouring positions
- step_count: int32 [1], replicated, may hold values from 2 to 4
- norm_gains: float32 [2, 2048], P(None, 'dp'), may hold values from 0.5 to 1.5
- gains_first: float32 [2, 2048], P(None, 'dp'), may hold values from -0.0004272461 to 0.0004272461
- gains_second: float32 [2, 2048], P(None, 'dp'), may hold values from 9.5358565e-09 to 1.5211961e-07
- w_query: float32 [2048, 2048], P('dp', 'tensor'), may hold values from -0.125 to 0.125
- query_first: float32 [2048, 2048], P('dp', 'tensor'), may hold values from -0.00015258789 to 0.00015258789
- query_second: float32 [2048, 2048], P('dp', 'tensor'), may hold values from 1.4757873e-09 to 2.3839641e-08
- w_keyval: float32 [2, 2048, 256], P(None, 'dp', 'tensor'), may hold values from -0.125 to 0.125
- keyval_first: float32 [2, 2048, 256], P(None, 'dp', 'tensor'), may hold values from -0.0004272461 to 0.0004272461
- keyval_second: float32 [2, 2048, 256], P(None, 'dp', 'tensor'), may hold values from 1.0353215e-08 to 1.6710453e-07
- w_out: float32 [2048, 2048], P('tensor', 'dp'), may hold values from -1.5 to 1.5
- out_first: float32 [2048, 2048], P('tensor', 'dp'), may hold values from -1.5258789e-05 to 1.5258789e-05
- out_second: float32 [2048, 2048], P('tensor', 'dp'), may hold values from 1.7709447e-11 to 2.860757e-10
- w_gateup: float32 [2, 2048, 5632], P(None, 'dp', 'tensor'), may hold values from -0.125 to 0.125
- gateup_first: float32 [2, 2048, 5632], P(None, 'dp', 'tensor'), may hold values from -5.340576e-05 to 5.340576e-05
- gateup_second: float32 [2, 2048, 5632], P(None, 'dp', 'tensor'), may hold values from 1.4757873e-10 to 2.3839641e-09
- w_down: float32 [5632, 2048], P('tensor', 'dp'), may hold values from -0.15625 to 0.15625
- down_first: float32 [5632, 2048], P('tensor', 'dp'), may hold values from -4.5776367e-05 to 4.5776367e-05
- down_second: float32 [5632, 2048], P('tensor', 'dp'), may hold values from 1.1806298e-10 to 1.9071713e-09
Outputs:
- layer_out: bfloat16 [8192, 2048], P('dp')
- input_grad: float32 [8192, 2048], P('dp')
- grad_norm: float32 [1], replicated
- gains_moment: float32 [2, 2048], P(None, 'dp')
- gains_square: float32 [2, 2048], P(None, 'dp')
- gains_new: float32 [2, 2048], P(None, 'dp')
- query_moment: float32 [2048, 2048], P('dp', 'tensor')
- query_square: float32 [2048, 2048], P('dp', 'tensor')
- query_new: float32 [2048, 2048], P('dp', 'tensor')
- keyval_moment: float32 [2, 2048, 256], P(None, 'dp', 'tensor')
- keyval_square: float32 [2, 2048, 256], P(None, 'dp', 'tensor')
- keyval_new: float32 [2, 2048, 256], P(None, 'dp', 'tensor')
- out_moment: float32 [2048, 2048], P('tensor', 'dp')
- out_square: float32 [2048, 2048], P('tensor', 'dp')
- out_new: float32 [2048, 2048], P('tensor', 'dp')
- gateup_moment: float32 [2, 2048, 5632], P(None, 'dp', 'tensor')
- gateup_square: float32 [2, 2048, 5632], P(None, 'dp', 'tensor')
- gateup_new: float32 [2, 2048, 5632], P(None, 'dp', 'tensor')
- down_moment: float32 [5632, 2048], P('tensor', 'dp')
- down_square: float32 [5632, 2048], P('tensor', 'dp')
- down_new: float32 [5632, 2048], P('tensor', 'dp')
Inputs may be any that keep to these rules, and one draw needn't show every extreme that they name: `segment_ids`: in each batch row the segment ids never fall, all 3 ids occur, and the longest sequence of a row has 768 tokens; a token attends to the earlier tokens of its own sequence only.
All inputs are finite; a program needn't handle non-finite values.
Results may differ from a plain program's by a relative error of at most 0.017.
Values may be sent and summed in bfloat16 or wider, within the bound.
A program may use at most 320 MiB of HBM per device.

v0:
```python
import jax
import jax.numpy as jnp
from jax import lax
from jax.sharding import PartitionSpec as P

HD = 64
norm_eps = 1e-05
beta_first = 0.9
beta_second = 0.95
adam_eps = 1e-08
weight_decay = 0.1
weight_rate = 0.02
out_rate = 0.1
gain_rate = 0.2
clip_limit = 1.0
masked_value = -1000000000.0


def positions(segment):
    length = segment.shape[0]
    indices = jnp.arange(length, dtype=jnp.int32)
    earlier = jnp.concatenate([segment[:1] - 1, segment[:-1]])
    begins = jnp.where(segment != earlier, indices, jnp.zeros_like(indices))
    return indices - lax.cummax(begins, axis=0)


def rotary_tables(places, width):
    half_width = width // 2
    frequency = jnp.power(10000.0, -jnp.arange(half_width, dtype=jnp.float32) * (2.0 / width))
    angles = places.astype(jnp.float32)[:, None] * frequency[None, :]
    cosine_table = jnp.concatenate([jnp.cos(angles), jnp.cos(angles)], axis=-1)
    sine_table = jnp.concatenate([jnp.sin(angles), jnp.sin(angles)], axis=-1)
    return (cosine_table, sine_table)


def rotate(values, cosine_table, sine_table):
    half_width = values.shape[-1] // 2
    turned = jnp.concatenate([-values[..., half_width:], values[..., :half_width]], axis=-1)
    return values * cosine_table[:, None, :] + turned * sine_table[:, None, :]


def unrotate(gradient, cosine_table, sine_table):
    half_width = gradient.shape[-1] // 2
    along_sine = gradient * sine_table[:, None, :]
    turned = jnp.concatenate([along_sine[..., half_width:], -along_sine[..., :half_width]], axis=-1)
    return gradient * cosine_table[:, None, :] + turned


def over_rows(left, right):
    return lax.dot_general(
        left, right, (((0,), (0,)), ((), ())), preferred_element_type=jnp.float32
    )


def against(left, right):
    return lax.dot_general(
        left, right, (((1,), (1,)), ((), ())), preferred_element_type=jnp.float32
    )


def norm_back(grad_output, unit_rows, inverse, gain):
    scaled = grad_output * gain
    gain_grad = jnp.sum(grad_output * unit_rows, axis=0)
    inner_mean = jnp.mean(scaled * unit_rows, axis=-1, keepdims=True)
    return (inverse * (scaled - unit_rows * inner_mean), gain_grad)


def adam_step(weight, first, second, gradient, clip_factor, step_float, step_rate, decay_rate):
    gradient = gradient * clip_factor
    first = beta_first * first + (1.0 - beta_first) * gradient
    second = beta_second * second + (1.0 - beta_second) * gradient * gradient
    correct_one = 1.0 - jnp.power(beta_first, step_float)
    correct_two = 1.0 - jnp.power(beta_second, step_float)
    update = first / correct_one / (jnp.sqrt(second / correct_two) + adam_eps)
    return (first, second, weight - step_rate * (update + decay_rate * weight))


def on_device(
    tokens,
    cotangent,
    segment_ids,
    step_count,
    norm_gains,
    gains_first,
    gains_second,
    w_query,
    query_first,
    query_second,
    w_keyval,
    keyval_first,
    keyval_second,
    w_out,
    out_first,
    out_second,
    w_gateup,
    gateup_first,
    gateup_second,
    w_down,
    down_first,
    down_second,
):
    gathered = (
        lax.all_gather(norm_gains.astype(jnp.bfloat16), "dp", axis=1, tiled=True),
        lax.all_gather(w_query.astype(jnp.bfloat16), "dp", axis=0, tiled=True),
        lax.all_gather(w_keyval.astype(jnp.bfloat16), "dp", axis=1, tiled=True),
        lax.all_gather(w_out.astype(jnp.bfloat16), "dp", axis=1, tiled=True),
        lax.all_gather(w_gateup.astype(jnp.bfloat16), "dp", axis=1, tiled=True),
        lax.all_gather(w_down.astype(jnp.bfloat16), "dp", axis=1, tiled=True),
    )
    gain_rows, query_weight, keyval_weight, out_weight, gateup_weight, down_weight = gathered
    gain_values = gain_rows.astype(jnp.float32)
    length = tokens.shape[0]
    segment = segment_ids[0]
    local_heads = query_weight.shape[1] // HD
    local_groups = keyval_weight.shape[2] // HD
    group_size = local_heads // local_groups
    cosine_table, sine_table = rotary_tables(positions(segment), HD)
    indices = jnp.arange(length, dtype=jnp.int32)
    block_rows = min(512, length)
    starts = jnp.arange(length // block_rows, dtype=jnp.int32) * block_rows
    inverse_scale = HD ** (-0.5)
    values_in = tokens.astype(jnp.float32)
    inverse_one = lax.rsqrt(jnp.mean(values_in * values_in, axis=-1, keepdims=True) + norm_eps)
    unit_one = values_in * inverse_one
    normed_one = (unit_one * gain_values[0]).astype(jnp.bfloat16)
    query_raw = jnp.dot(normed_one, query_weight, preferred_element_type=jnp.float32)
    queries = rotate(query_raw.reshape(length, local_heads, HD), cosine_table, sine_table).astype(
        jnp.bfloat16
    )
    queries = queries.reshape(length, local_groups, group_size, HD)
    keyval_raw = jnp.einsum(
        "nd,sdk->snk", normed_one, keyval_weight, preferred_element_type=jnp.float32
    )
    key_rows = rotate(
        keyval_raw[0].reshape(length, local_groups, HD), cosine_table, sine_table
    ).astype(jnp.bfloat16)
    value_rows = keyval_raw[1].reshape(length, local_groups, HD).astype(jnp.bfloat16)

    def block_scores(start):
        query_block = lax.dynamic_slice_in_dim(queries, start, block_rows, 0)
        segment_block = lax.dynamic_slice_in_dim(segment, start, block_rows, 0)
        row_index = start + jnp.arange(block_rows, dtype=jnp.int32)
        allowed = (segment_block[:, None] == segment[None, :]) & (
            row_index[:, None] >= indices[None, :]
        )
        raw_scores = jnp.einsum(
            "qkgh,pkh->kgqp", query_block, key_rows, preferred_element_type=jnp.float32
        )
        return (query_block, jnp.where(allowed, raw_scores * inverse_scale, masked_value))

    def forward_block(start):
        query_block, scaled = block_scores(start)
        highest = jnp.max(scaled, axis=-1, keepdims=True)
        lifted = jnp.exp(scaled - highest)
        row_total = jnp.sum(lifted, axis=-1, keepdims=True)
        soft_weights = (lifted / row_total).astype(jnp.bfloat16)
        mixed = jnp.einsum(
            "kgqp,pkh->qkgh", soft_weights, value_rows, preferred_element_type=jnp.float32
        )
        return (
            mixed.astype(jnp.bfloat16).reshape(block_rows, local_heads * HD),
            (highest + jnp.log(row_total))[..., 0],
        )

    mixed_blocks, logsum_blocks = lax.map(forward_block, starts)
    mixture = mixed_blocks.reshape(length, local_heads * HD)
    branch_partial = jnp.dot(mixture, out_weight, preferred_element_type=jnp.float32)
    branch = lax.psum(branch_partial, "tensor")
    middle = values_in + branch
    inverse_two = lax.rsqrt(jnp.mean(middle * middle, axis=-1, keepdims=True) + norm_eps)
    unit_two = middle * inverse_two
    normed_two = (unit_two * gain_values[1]).astype(jnp.bfloat16)
    gateup = jnp.einsum(
        "nd,sdf->snf", normed_two, gateup_weight, preferred_element_type=jnp.float32
    )
    hidden = (jax.nn.silu(gateup[0]) * gateup[1]).astype(jnp.bfloat16)
    feed_out = lax.psum(
        jnp.dot(hidden, down_weight, preferred_element_type=jnp.float32).astype(jnp.bfloat16),
        "tensor",
    ).astype(jnp.float32)
    layer_out = (middle + feed_out).astype(jnp.bfloat16)
    regathered = (
        lax.all_gather(norm_gains.astype(jnp.bfloat16), "dp", axis=1, tiled=True),
        lax.all_gather(w_query.astype(jnp.bfloat16), "dp", axis=0, tiled=True),
        lax.all_gather(w_keyval.astype(jnp.bfloat16), "dp", axis=1, tiled=True),
        lax.all_gather(w_out.astype(jnp.bfloat16), "dp", axis=1, tiled=True),
        lax.all_gather(w_gateup.astype(jnp.bfloat16), "dp", axis=1, tiled=True),
        lax.all_gather(w_down.astype(jnp.bfloat16), "dp", axis=1, tiled=True),
    )
    gain_rows, query_weight, keyval_weight, out_weight, gateup_weight, down_weight = regathered
    gain_values = gain_rows.astype(jnp.float32)
    grad_down_weight = over_rows(hidden, cotangent)
    grad_hidden = against(cotangent, down_weight)
    gate_values = gateup[0]
    up_values = gateup[1]
    sigmoid_gate = jax.nn.sigmoid(gate_values)
    grad_gate = grad_hidden * up_values * sigmoid_gate * (1.0 + gate_values * (1.0 - sigmoid_gate))
    grad_up = grad_hidden * gate_values * sigmoid_gate
    grad_gateup = jnp.stack([grad_gate, grad_up]).astype(jnp.bfloat16)
    grad_gateup_weight = jnp.einsum(
        "nd,snf->sdf", normed_two, grad_gateup, preferred_element_type=jnp.float32
    )
    partial_two = jnp.einsum(
        "snf,sdf->nd", grad_gateup, gateup_weight, preferred_element_type=jnp.float32
    )
    grad_normed_two = lax.psum(partial_two, "tensor")
    grad_from_two, gain_grad_two = norm_back(grad_normed_two, unit_two, inverse_two, gain_values[1])
    grad_middle = cotangent.astype(jnp.float32) + grad_from_two
    grad_branch = grad_middle.astype(jnp.bfloat16)
    grad_out_weight = over_rows(mixture, grad_branch)
    grad_mixture = (
        against(grad_branch, out_weight)
        .astype(jnp.bfloat16)
        .reshape(length, local_groups, group_size, HD)
    )

    def backward_block(carried, pieces):
        start, logsum = pieces
        query_block, scaled = block_scores(start)
        soft_weights = jnp.exp(scaled - logsum[..., None])
        grad_block = lax.dynamic_slice_in_dim(grad_mixture, start, block_rows, 0)
        grad_soft = jnp.einsum(
            "qkgh,pkh->kgqp", grad_block, value_rows, preferred_element_type=jnp.float32
        )
        spread = jnp.sum(soft_weights * grad_soft, axis=-1, keepdims=True)
        grad_scores = (soft_weights * (grad_soft - spread) * inverse_scale).astype(jnp.bfloat16)
        grad_query = jnp.einsum(
            "kgqp,pkh->qkgh", grad_scores, key_rows, preferred_element_type=jnp.float32
        )
        grad_key = carried[0] + jnp.einsum(
            "kgqp,qkgh->pkh", grad_scores, query_block, preferred_element_type=jnp.float32
        )
        grad_value = carried[1] + jnp.einsum(
            "kgqp,qkgh->pkh",
            soft_weights.astype(jnp.bfloat16),
            grad_block,
            preferred_element_type=jnp.float32,
        )
        return ((grad_key, grad_value), grad_query)

    zero_rows = jnp.zeros((length, local_groups, HD), jnp.float32)
    (grad_keys, grad_values), grad_queries = lax.scan(
        backward_block, (zero_rows, zero_rows), (starts, logsum_blocks)
    )
    grad_queries = grad_queries.reshape(length, local_heads, HD)
    grad_query_raw = (
        unrotate(grad_queries, cosine_table, sine_table)
        .astype(jnp.bfloat16)
        .reshape(length, local_heads * HD)
    )
    grad_key_raw = unrotate(grad_keys, cosine_table, sine_table).reshape(length, local_groups * HD)
    grad_keyval = jnp.stack([grad_key_raw, grad_values.reshape(length, local_groups * HD)]).astype(
        jnp.bfloat16
    )
    grad_query_weight = over_rows(normed_one, grad_query_raw)
    grad_keyval_weight = jnp.einsum(
        "nd,snk->sdk", normed_one, grad_keyval, preferred_element_type=jnp.float32
    )
    partial_one = against(grad_query_raw, query_weight) + jnp.einsum(
        "snk,sdk->nd", grad_keyval, keyval_weight, preferred_element_type=jnp.float32
    )
    grad_normed_one = lax.psum(partial_one.astype(jnp.bfloat16), "tensor").astype(jnp.float32)
    grad_from_one, gain_grad_one = norm_back(grad_normed_one, unit_one, inverse_one, gain_values[0])
    input_grad = grad_middle + grad_from_one
    gain_grads = jnp.stack([gain_grad_one, gain_grad_two])
    reduced = (
        lax.psum_scatter(gain_grads, "dp", scatter_dimension=1, tiled=True),
        lax.psum_scatter(grad_query_weight, "dp", scatter_dimension=0, tiled=True),
        lax.psum_scatter(grad_keyval_weight, "dp", scatter_dimension=1, tiled=True),
        lax.psum_scatter(grad_out_weight, "dp", scatter_dimension=1, tiled=True),
        lax.psum_scatter(grad_gateup_weight, "dp", scatter_dimension=1, tiled=True),
        lax.psum_scatter(grad_down_weight, "dp", scatter_dimension=1, tiled=True),
    )
    first_owner = (lax.axis_index("tensor") == 0).astype(jnp.float32)
    local_square = first_owner * jnp.sum(reduced[0] * reduced[0]) + sum(
        (jnp.sum(g * g) for g in reduced[1:])
    )
    square_total = lax.psum(local_square, ("dp", "tensor"))
    grad_norm = jnp.sqrt(square_total)
    clip_factor = jnp.minimum(1.0, clip_limit / (grad_norm + 1e-06))
    step_float = step_count[0].astype(jnp.float32)
    params = (norm_gains, w_query, w_keyval, w_out, w_gateup, w_down)
    states = (
        (gains_first, gains_second),
        (query_first, query_second),
        (keyval_first, keyval_second),
        (out_first, out_second),
        (gateup_first, gateup_second),
        (down_first, down_second),
    )
    step_rates = (gain_rate, weight_rate, weight_rate, out_rate, weight_rate, weight_rate)
    decay_rates = (0.0, weight_decay, weight_decay, weight_decay, weight_decay, weight_decay)
    results = []
    for position_index in range(6):
        first, second = states[position_index]
        results.extend(
            adam_step(
                params[position_index],
                first,
                second,
                reduced[position_index],
                clip_factor,
                step_float,
                step_rates[position_index],
                decay_rates[position_index],
            )
        )
    return (
        layer_out,
        input_grad,
        grad_norm.reshape(1),
        results[0],
        results[1],
        results[2],
        results[3],
        results[4],
        results[5],
        results[6],
        results[7],
        results[8],
        results[9],
        results[10],
        results[11],
        results[12],
        results[13],
        results[14],
        results[15],
        results[16],
        results[17],
    )


def solution(mesh):
    in_specs = (
        P("dp", None),
        P("dp", None),
        P("dp", None),
        P(),
        P(None, "dp"),
        P(None, "dp"),
        P(None, "dp"),
        P("dp", "tensor"),
        P("dp", "tensor"),
        P("dp", "tensor"),
        P(None, "dp", "tensor"),
        P(None, "dp", "tensor"),
        P(None, "dp", "tensor"),
        P("tensor", "dp"),
        P("tensor", "dp"),
        P("tensor", "dp"),
        P(None, "dp", "tensor"),
        P(None, "dp", "tensor"),
        P(None, "dp", "tensor"),
        P("tensor", "dp"),
        P("tensor", "dp"),
        P("tensor", "dp"),
    )
    out_specs = (
        P("dp", None),
        P("dp", None),
        P(),
        P(None, "dp"),
        P(None, "dp"),
        P(None, "dp"),
        P("dp", "tensor"),
        P("dp", "tensor"),
        P("dp", "tensor"),
        P(None, "dp", "tensor"),
        P(None, "dp", "tensor"),
        P(None, "dp", "tensor"),
        P("tensor", "dp"),
        P("tensor", "dp"),
        P("tensor", "dp"),
        P(None, "dp", "tensor"),
        P(None, "dp", "tensor"),
        P(None, "dp", "tensor"),
        P("tensor", "dp"),
        P("tensor", "dp"),
        P("tensor", "dp"),
    )
    return jax.shard_map(
        on_device, mesh=mesh, in_specs=in_specs, out_specs=out_specs, check_vma=False
    )
```

profile of v0, /device:TPU:0, one launch (start us, length us, event | category | flops | bytes accessed | tf_op | source)
XLA Modules:
  0.0 1800.6 jit_solution(3728736641630619204)
XLA Ops:
  11.8 10.5 all_gather.24
  22.9 3.1 fusion.64
  26.0 14.2 all_gather.26
  45.1 5.4 fusion.111
  51.2 37.7 %while.28 = (s32[]{:T(128)}, bf16[2,512,512]{2,1,0:T(8,128)(2,1)}, f32[2,1,8,512]{3,2,1,0:T(8,128)}, s32[2]{0:T(128)S(1)}, s32[1024]{0:T(1024)S(1)}, /*index=5*/...) while((s32[]{:T(128)}, bf16[2,512,512]{2,1,0:T(8,128)(2,1)}, ...), condition=%wide.region_6.7_spmd.clone, body=%wide.region_3.6_spmd.clone.sunk | while | flops 1125904896 | bytes 64371432 | solution.py:165
  55.6 3.1 fusion.168
  58.7 4.4 fusion.169
  63.7 5.3 fusion.170
  74.2 3.2 fusion.168
  77.3 4.4 fusion.169
  82.3 5.3 fusion.170
  88.9 7.7 fusion.122
  96.7 3.2 convert_element_type.148
  100.9 287.2 %all-reduce.5.cloned.1.call-done = f32[1024,2048]{1,0:T(8,128)} async-done(((f32[1024,2048]{1,0:T(8,128)}), f32[1024,2048]{1,0:T(8,128)}) %all-reduce.5.cloned.1.call-update) | async-done | bytes 8388624 | tf_op jit(solution)/shard_map/psum | solution.py:168
  388.1 9.2 multiply_reduce_fusion.2
  397.4 59.8 %all-gather.9.cloned.1.call-done = bf16[2,2048,1408]{2,1,0:T(8,128)(2,1)} async-done(((bf16[2,256,1408]{2,1,0:T(8,128)(2,1)}), bf16[2,2048,1408]{2,1,0:T(8,128)(2,1)}) %all-gather.9.cloned.1.call-update) | async-done | bytes 11534352 | tf_op jit(solution)/shard_map/all_gather | solution.py:107
  457.2 20.2 %convolution_bitcast_fusion.3 = f32[2,1024,1408]{2,1,0:T(8,128)} fusion(bf16[2,2048,1408]{2,1,0:T(8,128)(2,1)} %all-gather.9.cloned.1.call-done, f32[1024,2048]{1,0:T(8,128)} %get-tuple-element.339, f32[2048]{0:T(1024)S(1)} %bitcast.364, f32[1024]{0:T(1024)S(1)} %add_rsqrt_fusion), kind=kOutput, calls=%fused_computation.85 | convolution fusion | flops 11817451520 | bytes 31469568 | tf_op jit(solution)/shard_map/nd,sdf->snf/dot_general | solution.py:173
  477.4 26.5 %all-gather.11.cloned.1.call-done = bf16[1408,2048]{1,0:T(8,128)(2,1)} async-done(((bf16[1408,256]{1,0:T(8,128)(2,1)}), bf16[1408,2048]{1,0:T(8,128)(2,1)}) %all-gather.11.cloned.1.call-update) | async-done | bytes 5767184 | tf_op jit(solution)/shard_map/all_gather | solution.py:108
  503.9 15.6 fusion.71
  522.0 17.0 convolution_bitcast_fusion.4
  539.1 11.3 convolution_convert_fusion
  550.4 279.6 %all-reduce.7.cloned.1.call-done = f32[1024,2048]{1,0:T(8,128)} async-done(((f32[1024,2048]{1,0:T(8,128)}), f32[1024,2048]{1,0:T(8,128)}) %all-reduce.7.cloned.1.call-update) | async-done | bytes 8388624 | tf_op jit(solution)/shard_map/psum | solution.py:206
  830.0 7.6 multiply_reduce_fusion
  839.5 4.7 multiply_add_fusion
  844.2 3.4 copy-done.1
  847.6 3.3 fusion.82
  850.9 129.5 %while.29 = (s32[]{:T(128)}, f32[1024,1,64]{0,2,1:T(8,128)}, f32[1024,1,64]{0,2,1:T(8,128)}, f32[2,512,1,8,64]{1,0,4,3,2:T(2,128)}, s32[2]{0:T(128)S(1)}, /*inde...) while((s32[]{:T(128)}, f32[1024,1,64]{0,2,1:T(8,128)}, ...), condition=%wide.region_14.15_spmd.clone, body=%wide.region_12.14_spmd.clone.sunk | while | flops 2728129024 | bytes 178878960 | solution.py:242
  855.6 3.6 fusion.179
  859.7 10.8 fusion.181
  870.5 7.3 fusion.182
  877.8 3.7 convolution_bitcast_fusion.6
  882.7 19.5 %dynamic_update_slice.22 = f32[2,512,1,8,64]{1,0,4,3,2:T(2,128)} dynamic-update-slice(f32[2,512,1,8,64]{1,0,4,3,2:T(2,128)} %get-tuple-element.553, f32[1,512,1,8,64]{1,0,4,3,2:T(1,128)S(1)} %copy.99, s32[]{:T(128)} %get-tuple-element.550, s32[]{:T(128)} %constant.54.clone.1..sunk.1, s32[]{:T(128)} %constant.54.clone.1..sunk.1, s32[]{:T(128)} %constant.54.clone.1..sunk.1, s32[]{:T(128)} %constant.54.clone.1..sunk.1) | dynamic-update-slice | bytes 2097156 | tf_op jit(solution)/shard_map/while/body/jit(dynamic_update_index_in_dim)/dynamic_update_slice | solution.py:242
  902.2 5.2 fusion.183
  907.4 7.5 fusion.184
  920.3 3.5 fusion.179
  924.4 10.8 fusion.181
  935.2 7.3 fusion.182
  942.5 3.7 convolution_bitcast_fusion.6
  947.4 19.5 %dynamic_update_slice.22 = f32[2,512,1,8,64]{1,0,4,3,2:T(2,128)} dynamic-update-slice(f32[2,512,1,8,64]{1,0,4,3,2:T(2,128)} %get-tuple-element.553, f32[1,512,1,8,64]{1,0,4,3,2:T(1,128)S(1)} %copy.99, s32[]{:T(128)} %get-tuple-element.550, s32[]{:T(128)} %constant.54.clone.1..sunk.1, s32[]{:T(128)} %constant.54.clone.1..sunk.1, s32[]{:T(128)} %constant.54.clone.1..sunk.1, s32[]{:T(128)} %constant.54.clone.1..sunk.1) | dynamic-update-slice | bytes 2097156 | tf_op jit(solution)/shard_map/while/body/jit(dynamic_update_index_in_dim)/dynamic_update_slice | solution.py:242
  966.9 5.2 fusion.183
  972.1 7.6 fusion.184
  982.5 3.2 reshape.481
  991.9 3.3 fusion.65
  995.9 4.6 fusion.72
  1000.5 6.9 fusion.107
  1008.6 7.8 fusion.78
  1016.5 269.4 %all-reduce.9.cloned.1.call-done = (bf16[1024,2048]{1,0:T(8,128)(2,1)}, bf16[1024,2048]{1,0:T(8,128)(2,1)}) async-done(((bf16[1024,2048]{1,0:T(8,128)(2,1)}, bf16[1024,2048]{1,0:T(8,128)(2,1)}), (bf16[1024,2048]{1,0:T(8,128)(2,1)}, bf16[1024,2048]{1,0:T(8,128)(2,1)})) %all-reduce.9.cloned.1.call-update) | async-done | bytes 8388624 | tf_op jit(solution)/shard_map/psum | solution.py:177
  1285.9 5.0 fusion.63
  1292.4 11.3 fusion.124
  1304.4 21.0 %convolution_bitcast_fusion.2 = f32[2,2048,1408]{1,2,0:T(8,128)} fusion(bf16[1,1024,1408]{2,1,0:T(8,128)(2,1)} %copy-done.62, bf16[1,1024,1408]{2,1,0:T(8,128)(2,1)} %copy-done.61, f32[1024,2048]{1,0:T(8,128)} %get-tuple-element.339, f32[2048]{0:T(1024)S(1)} %bitcast.367, f32[1024]{0:T(1024)S(1)} %copy-done.52), kind=kOutput, calls=%fused_computation.61 | convolution fusion | flops 11820335104 | bytes 37236736 | tf_op jit(solution)/shard_map/nd,snf->sdf/dot_general | solution.py:200
  1330.3 3.4 copy.68
  1337.5 42.0 %reduce-scatter.9.cloned.1.call-done = f32[256,512]{1,0:T(8,128)} async-done(((f32[2048,512]{1,0:T(8,128)}), f32[256,512]{1,0:T(8,128)}) %reduce-scatter.9.cloned.1.call-update) | async-done | bytes 524304 | tf_op jit(solution)/shard_map/reduce_scatter | solution.py:268
  1382.5 51.9 %reduce-scatter.13.cloned.1.call-done = f32[512,256]{1,0:T(8,128)} async-done(((f32[512,2048]{1,0:T(8,128)}), f32[512,256]{1,0:T(8,128)}) %reduce-scatter.13.cloned.1.call-update) | async-done | bytes 524304 | tf_op jit(solution)/shard_map/reduce_scatter | solution.py:270
  1436.8 9.5 fusion.60
  1446.3 27.9 %reduce-scatter.19.cloned.1.call-done = f32[256,2]{1,0:T(8,128)} async-done(((f32[2048,2]{1,0:T(8,128)}), f32[256,2]{1,0:T(8,128)}) %reduce-scatter.19.cloned.1.call-update) | async-done | bytes 2064
  1476.4 87.9 %reduce-scatter.17.cloned.1.call-done = f32[1408,256]{1,0:T(8,128)} async-done(((f32[1408,2048]{1,0:T(8,128)}), f32[1408,256]{1,0:T(8,128)}) %reduce-scatter.17.cloned.1.call-update) | async-done | bytes 1441808 | tf_op jit(solution)/shard_map/reduce_scatter | solution.py:272
  1566.7 147.2 %reduce-scatter.15.cloned.1.call-done = f32[2,256,1408]{1,2,0:T(8,128)} async-done(((f32[2,2048,1408]{1,2,0:T(8,128)}), f32[2,256,1408]{1,2,0:T(8,128)}) %reduce-scatter.15.cloned.1.call-update) | async-done | bytes 2883600 | tf_op jit(solution)/shard_map/reduce_scatter | solution.py:271
  1713.9 3.2 multiply_reduce_fusion.3
  1718.4 8.4 add_convert_fusion
  1726.8 39.5 %psum.39 = f32[]{:T(128)} all-reduce(f32[]{:T(128)S(6)} %add.273), channel_id=1, replica_groups=mesh['dp'=8,'tensor'=4] {'dp','tensor'}, use_global_device_ids=true, to_apply=%region_31.32 | all-reduce | flops 1 | bytes 8 | tf_op jit(solution)/shard_map/psum | solution.py:278
  1767.1 6.3 multiply_subtract_fusion
  1773.4 3.4 copy.72
  1776.8 3.5 copy.73
  1783.2 5.5 multiply_subtract_fusion.1
  (260 shorter events, 67.3 us)
Async XLA Ops:
  7.2 18.8 %copy-start.37 = (f32[2,256,64]{1,2,0:T(8,128)S(1)}, f32[2,256,64]{1,2,0:T(8,128)}, u32[]{:S(2)}) copy-start(f32[2,256,64]{1,2,0:T(8,128)} %param.36) | copy-start | bytes 393220
  7.2 37.9 %all-gather.5.cloned.1.call-start = ((), (), s32[]{:S(2)}) async-start(), calls=%async_computation.6 | async-start | bytes 2359296 | tf_op jit(solution)/shard_map/all_gather | solution.py:104
  9.1 79.8 %all-gather.7.cloned.1.call-start = ((), (), s32[]{:S(2)}) async-start(), calls=%async_computation.7 | async-start | bytes 2359296 | tf_op jit(solution)/shard_map/all_gather | solution.py:106
  10.9 377.2 %all-reduce.5.cloned.1.call-start = ((), (), s32[]{:S(2)}) async-start(), calls=%async_computation.8 | async-start | bytes 16777216 | tf_op jit(solution)/shard_map/psum | solution.py:168
  11.0 29.3 %copy-start.2 = (bf16[1024,2048]{1,0:T(8,128)(2,1)S(1)}, bf16[1024,2048]{1,0:T(8,128)(2,1)}, u32[]{:S(2)}) copy-start(bf16[1024,2048]{1,0:T(8,128)(2,1)} %param.26) | copy-start | bytes 12582916
  22.9 22.1 %copy-start.47 = (f32[1,2048]{1,0:T(1,128)}, f32[1,2048]{1,0:T(1,128)S(1)}, u32[]{:S(2)}) copy-start(f32[1,2048]{1,0:T(1,128)S(1)} %get-tuple-element.356) | copy-start | bytes 24580
  26.0 19.0 %copy-start.53 = (f32[1024]{0:T(1024)}, f32[1024]{0:T(1024)S(1)}, u32[]{:S(2)}) copy-start(f32[1024]{0:T(1024)S(1)} %add_rsqrt_fusion.1) | copy-start | bytes 12292
  44.3 6.1 copy-start.32
  44.4 6.2 copy-start.20
  44.4 6.2 copy-start.22
  63.7 5.6 copy-start.34
  82.3 5.6 copy-start.34
  88.9 7.7 copy-start.17
  96.6 3.3 copy-start.16
  96.6 360.6 %all-gather.9.cloned.1.call-start = ((), (), s32[]{:S(2)}) async-start(), calls=%async_computation.9 | async-start | bytes 12976128 | tf_op jit(solution)/shard_map/all_gather | solution.py:107
  99.9 404.0 %all-gather.11.cloned.1.call-start = ((), (), s32[]{:S(2)}) async-start(), calls=%async_computation.10 | async-start | bytes 6488064 | tf_op jit(solution)/shard_map/all_gather | solution.py:108
  100.9 356.3 %copy-start.49 = (f32[1,2048]{1,0:T(1,128)S(1)}, f32[1,2048]{1,0:T(1,128)}, u32[]{:S(2)}) copy-start(f32[1,2048]{1,0:T(1,128)} %get-tuple-element.355) | copy-start | bytes 24580
  100.9 729.1 %all-reduce.7.cloned.1.call-start = ((), (), s32[]{:S(2)}) async-start(), calls=%async_computation.11 | async-start | bytes 16777216 | tf_op jit(solution)/shard_map/psum | solution.py:206
  397.4 440.3 %copy-start.51 = (f32[1024]{0:T(1024)}, f32[1024]{0:T(1024)S(1)}, u32[]{:S(2)}) copy-start(f32[1024]{0:T(1024)S(1)} %add_rsqrt_fusion) | copy-start | bytes 12292
  519.5 2.5 copy-start.62
  539.1 746.9 %all-reduce.9.cloned.1.call-start = ((), (), s32[]{:S(2)}) async-start(), calls=%async_computation.18 | async-start | bytes 16777216 | tf_op jit(solution)/shard_map/psum | solution.py:177
  830.0 8.2 copy-start.5
  830.0 9.4 copy-start.18
  839.5 8.1 copy-start.60
  844.2 3.4 copy-start.1
  850.9 4.6 copy-start.3
  855.6 3.6 copy-start.44
  877.8 3.7 copy-start
  881.6 20.6 %copy-start.7 = (f32[1024,1,64]{0,2,1:T(8,128)S(1)}, f32[1024,1,64]{0,2,1:T(8,128)}, u32[]{:S(2)}) copy-start(f32[1024,1,64]{0,2,1:T(8,128)} %get-tuple-element.551) | copy-start | bytes 786436 | tf_op jit(solution)/shard_map/while
  902.2 5.2 copy-start.6
  902.2 5.2 copy-start.13
  907.4 7.6 copy-start.8
  907.4 8.3 copy-start.4
  915.7 4.6 copy-start.3
  920.3 3.5 copy-start.44
  942.5 3.7 copy-start
  946.3 20.6 %copy-start.7 = (f32[1024,1,64]{0,2,1:T(8,128)S(1)}, f32[1024,1,64]{0,2,1:T(8,128)}, u32[]{:S(2)}) copy-start(f32[1024,1,64]{0,2,1:T(8,128)} %get-tuple-element.551) | copy-start | bytes 786436 | tf_op jit(solution)/shard_map/while
  966.9 5.2 copy-start.6
  966.9 5.2 copy-start.13
  972.1 7.6 copy-start.8
  972.1 8.3 copy-start.4
  980.4 5.4 copy-start.21
  989.5 2.4 copy-start.25
  995.2 340.7 %reduce-scatter.11.cloned.1.call-start = ((), (), s32[]{:S(2)}) async-start(), calls=%async_computation.13 | async-start | bytes 1179648 | tf_op jit(solution)/shard_map/reduce_scatter | solution.py:269
  1000.5 379.0 %reduce-scatter.9.cloned.1.call-start = ((), (), s32[]{:S(2)}) async-start(), calls=%async_computation.12 | async-start | bytes 4718592 | tf_op jit(solution)/shard_map/reduce_scatter | solution.py:268
  1007.4 427.0 %reduce-scatter.13.cloned.1.call-start = ((), (), s32[]{:S(2)}) async-start(), calls=%async_computation.14 | async-start | bytes 4718592 | tf_op jit(solution)/shard_map/reduce_scatter | solution.py:270
  1016.5 457.7 %reduce-scatter.19.cloned.1.call-start = ((), (), s32[]{:S(2)}) async-start(), calls=%async_computation.17 | async-start | bytes 1179648
  1285.9 5.0 copy-start.55
  1292.3 272.0 %reduce-scatter.17.cloned.1.call-start = ((), (), s32[]{:S(2)}) async-start(), calls=%async_computation.16 | async-start | bytes 12976128 | tf_op jit(solution)/shard_map/reduce_scatter | solution.py:272
  1303.8 410.1 %reduce-scatter.15.cloned.1.call-start = ((), (), s32[]{:S(2)}) async-start(), calls=%async_computation.15 | async-start | bytes 25952256 | tf_op jit(solution)/shard_map/reduce_scatter | solution.py:271
  1329.4 4.3 copy-start.19
  1718.4 48.7 %copy-start.10 = (f32[2,256,1408]{1,2,0:T(8,128)S(1)}, f32[2,256,1408]{1,2,0:T(8,128)}, u32[]{:S(2)}) copy-start(f32[2,256,1408]{1,2,0:T(8,128)} %reduce-scatter.15.cloned.1.call-done) | copy-start | bytes 8650756
  1776.8 3.5 copy-start.11
  1783.2 5.6 copy-start.26
  1783.2 5.6 copy-start.29
  1783.2 5.6 copy-start.40
  1783.2 5.6 copy-start.41
  1783.2 7.1 copy-start.38
  1783.2 7.0 copy-start.39
  1783.2 7.0 copy-start.45
  1783.2 7.0 copy-start.46
  1788.8 2.3 copy-start.27
  1788.8 2.2 copy-start.28
  1788.8 2.2 copy-start.42
  (23 other events, 31.5 us)
Sparse Core Ops, SparseCore 0:
  10.5 32.9 all-gather.4
  45.9 28.5 all-gather.6
  96.7 291.3 all-reduce.4
  390.5 66.6 all-gather.8
  459.5 44.3 all-gather.10
  539.2 290.8 all-reduce.6
  995.4 290.5 all-reduce.8
  1289.7 35.0 reduce-scatter.10
  1328.1 51.2 reduce-scatter.8
  1383.0 51.3 reduce-scatter.12
  1438.2 35.9 reduce-scatter.18
  1477.5 86.7 reduce-scatter.16
  1568.0 145.8 reduce-scatter.14
where the time goes:
time: 1810 us; the launch traced here: 1800 us
  waiting for transfers between devices  1280 us (71%)
  matrix products  218 us (12%)
  other arithmetic  120 us (7%)
  local copies, waits for them, and re-layouts  87.9 us (5%)
  blocking collectives  64.2 us (4%)
  between operations  22.3 us (1%)
    psum x1, waiting for transfers between devices, on_device(): branch = lax.psum(branch_partial, 'tensor')  287 us
    psum x1, waiting for transfers between devices, on_device(): grad_normed_two = lax.psum(partial_two, 'tensor')  280 us
    psum x1, waiting for transfers between devices, on_device(): lax.psum(jnp.dot(hidden, down_weight, preferred_element_type=jnp.float32)...  269 us
    reduce_scatter x1, waiting for transfers between devices, on_device(): lax.psum_scatter(grad_gateup_weight, 'dp', scatter_dimension=1, tiled=True)  147 us
    reduce_scatter x1, waiting for transfers between devices, on_device(): lax.psum_scatter(grad_down_weight, 'dp', scatter_dimension=1, tiled=True)  87.9 us
    all_gather x1, waiting for transfers between devices, on_device(): lax.all_gather(w_gateup.astype(jnp.bfloat16), 'dp', axis=1, tiled=True)  59.8 us
    reduce_scatter x1, waiting for transfers between devices, on_device(): lax.psum_scatter(grad_out_weight, 'dp', scatter_dimension=1, tiled=True)  51.9 us
    reduce_scatter x1, waiting for transfers between devices, on_device(): lax.psum_scatter(grad_query_weight, 'dp', scatter_dimension=0, tiled=True)  42 us
  transfers between devices with their start and end apart: 13, of which 10 were waited for; matrix products, arithmetic and copies ran while one was open for 10% of the time, Pallas kernels for 0%

commit v1 on v0

--- a/solution.py
+++ b/solution.py
@@ -275,7 +275,7 @@
     local_square = first_owner * jnp.sum(reduced[0] * reduced[0]) + sum(
         (jnp.sum(g * g) for g in reduced[1:])
     )
-    square_total = lax.psum(local_square, ("dp", "tensor"))
+    square_total = lax.psum(lax.psum(local_square, "tensor"), "dp")
     grad_norm = jnp.sqrt(square_total)
     clip_factor = jnp.minimum(1.0, clip_limit / (grad_norm + 1e-06))
     step_float = step_count[0].astype(jnp.float32)

time: 1810 us -> 1800 us (level)
    psum x1 -> x2, blocking collectives: 39.5 us -> 24.8 us  [on_device(): square_total = lax.psum(lax.psum(local_square, 'tensor'), 'dp')]
  transfers between devices with their start and end apart: 13 -> 13, of which waited for: 10 -> 10; matrix products, arithmetic and copies ran while one was open for 10% -> 9% of each run, Pallas kernels for 0% -> 0%
where the time goes in v1:
time: 1800 us; the launch traced here: 1790 us
  waiting for transfers between devices  1290 us (72%)
  matrix products  218 us (12%)
  other arithmetic  120 us (7%)
  local copies, waits for them, and re-layouts  85.7 us (5%)
  blocking collectives  49.5 us (3%)
  between operations  22.2 us (1%)
    psum x1, waiting for transfers between devices, on_device(): branch = lax.psum(branch_partial, 'tensor')  287 us
    psum x1, waiting for transfers between devices, on_device(): grad_normed_two = lax.psum(partial_two, 'tensor')  280 us
    psum x1, waiting for transfers between devices, on_device(): lax.psum(jnp.dot(hidden, down_weight, preferred_element_type=jnp.float32)...  269 us
    reduce_scatter x1, waiting for transfers between devices, on_device(): lax.psum_scatter(grad_gateup_weight, 'dp', scatter_dimension=1, tiled=True)  147 us
    reduce_scatter x1, waiting for transfers between devices, on_device(): lax.psum_scatter(grad_down_weight, 'dp', scatter_dimension=1, tiled=True)  87.9 us
    all_gather x1, waiting for transfers between devices, on_device(): lax.all_gather(w_gateup.astype(jnp.bfloat16), 'dp', axis=1, tiled=True)  59.8 us
    reduce_scatter x1, waiting for transfers between devices, on_device(): lax.psum_scatter(grad_out_weight, 'dp', scatter_dimension=1, tiled=True)  51.8 us
    reduce_scatter x1, waiting for transfers between devices, on_device(): lax.psum_scatter(grad_query_weight, 'dp', scatter_dimension=0, tiled=True)  41.6 us
  transfers between devices with their start and end apart: 13, of which 10 were waited for; matrix products, arithmetic and copies ran while one was open for 9% of the time, Pallas kernels for 0%

profile of v1, /device:TPU:0, one launch (start us, length us, event | category | flops | bytes accessed | tf_op | source)
XLA Modules:
  0.0 1793.7 jit_solution(14061763398037035738)
XLA Ops:
  11.8 10.5 all_gather.24
  26.0 14.2 all_gather.26
  45.0 5.3 fusion.111
  51.2 35.8 %while.28 = (s32[]{:T(128)}, bf16[2,512,512]{2,1,0:T(8,128)(2,1)S(1)}, f32[2,1,8,512]{3,2,1,0:T(8,128)}, s32[2]{0:T(128)S(1)}, s32[1024]{0:T(1024)S(1)}, /*index...) while((s32[]{:T(128)}, ...), condition=%wide.region_6.7_spmd.clone, body=%wide.region_3.6_spmd.clone.sunk | while | flops 1125904896 | bytes 55982772 | solution.py:165
  55.6 3.2 fusion.168
  58.7 4.4 fusion.169
  63.7 5.3 fusion.170
  73.2 3.2 fusion.168
  76.4 4.4 fusion.169
  81.4 5.3 fusion.170
  87.0 7.7 fusion.122
  99.1 287.1 %all-reduce.5.cloned.1.call-done = f32[1024,2048]{1,0:T(8,128)} async-done(((f32[1024,2048]{1,0:T(8,128)}), f32[1024,2048]{1,0:T(8,128)}) %all-reduce.5.cloned.1.call-update) | async-done | bytes 8388624 | tf_op jit(solution)/shard_map/psum | solution.py:168
  386.2 9.2 multiply_reduce_fusion.2
  395.5 59.8 %all-gather.9.cloned.1.call-done = bf16[2,2048,1408]{2,1,0:T(8,128)(2,1)} async-done(((bf16[2,256,1408]{2,1,0:T(8,128)(2,1)}), bf16[2,2048,1408]{2,1,0:T(8,128)(2,1)}) %all-gather.9.cloned.1.call-update) | async-done | bytes 11534352 | tf_op jit(solution)/shard_map/all_gather | solution.py:107
  455.3 20.2 %convolution_bitcast_fusion.3 = f32[2,1024,1408]{2,1,0:T(8,128)} fusion(bf16[2,2048,1408]{2,1,0:T(8,128)(2,1)} %all-gather.9.cloned.1.call-done, f32[1024,2048]{1,0:T(8,128)} %get-tuple-element.339, f32[2048]{0:T(1024)S(1)} %bitcast.364, f32[1024]{0:T(1024)S(1)} %add_rsqrt_fusion), kind=kOutput, calls=%fused_computation.85 | convolution fusion | flops 11817451520 | bytes 31469568 | tf_op jit(solution)/shard_map/nd,sdf->snf/dot_general | solution.py:173
  475.5 26.5 %all-gather.11.cloned.1.call-done = bf16[1408,2048]{1,0:T(8,128)(2,1)} async-done(((bf16[1408,256]{1,0:T(8,128)(2,1)}), bf16[1408,2048]{1,0:T(8,128)(2,1)}) %all-gather.11.cloned.1.call-update) | async-done | bytes 5767184 | tf_op jit(solution)/shard_map/all_gather | solution.py:108
  502.0 15.6 fusion.71
  520.2 17.0 convolution_bitcast_fusion.4
  537.2 11.3 convolution_convert_fusion
  548.5 279.7 %all-reduce.7.cloned.1.call-done = f32[1024,2048]{1,0:T(8,128)} async-done(((f32[1024,2048]{1,0:T(8,128)}), f32[1024,2048]{1,0:T(8,128)}) %all-reduce.7.cloned.1.call-update) | async-done | bytes 8388624 | tf_op jit(solution)/shard_map/psum | solution.py:206
  828.2 7.6 multiply_reduce_fusion
  837.6 4.7 multiply_add_fusion
  842.3 3.7 fusion.82
  846.1 130.8 %while.29 = (s32[]{:T(128)}, f32[1024,1,64]{0,2,1:T(8,128)}, f32[1024,1,64]{0,2,1:T(8,128)}, f32[2,512,1,8,64]{1,0,4,3,2:T(2,128)}, s32[2]{0:T(128)S(1)}, /*inde...) while((s32[]{:T(128)}, f32[1024,1,64]{0,2,1:T(8,128)}, ...), condition=%wide.region_14.15_spmd.clone, body=%wide.region_12.14_spmd.clone.sunk | while | flops 2728129024 | bytes 178747856 | solution.py:242
  850.7 3.5 fusion.179
  855.6 10.8 fusion.181
  866.4 7.3 fusion.182
  873.7 3.7 convolution_bitcast_fusion.6
  878.5 19.5 %dynamic_update_slice.22 = f32[2,512,1,8,64]{1,0,4,3,2:T(2,128)} dynamic-update-slice(f32[2,512,1,8,64]{1,0,4,3,2:T(2,128)} %get-tuple-element.553, f32[1,512,1,8,64]{1,0,4,3,2:T(1,128)S(1)} %copy.99, s32[]{:T(128)} %get-tuple-element.550, s32[]{:T(128)} %constant.54.clone.1..sunk.1, s32[]{:T(128)} %constant.54.clone.1..sunk.1, s32[]{:T(128)} %constant.54.clone.1..sunk.1, s32[]{:T(128)} %constant.54.clone.1..sunk.1) | dynamic-update-slice | bytes 2097156 | tf_op jit(solution)/shard_map/while/body/jit(dynamic_update_index_in_dim)/dynamic_update_slice | solution.py:242
  898.0 5.2 fusion.183
  903.2 7.5 fusion.184
  916.1 3.5 fusion.179
  921.0 10.8 fusion.181
  931.7 7.3 fusion.182
  939.1 3.7 convolution_bitcast_fusion.6
  943.9 19.5 %dynamic_update_slice.22 = f32[2,512,1,8,64]{1,0,4,3,2:T(2,128)} dynamic-update-slice(f32[2,512,1,8,64]{1,0,4,3,2:T(2,128)} %get-tuple-element.553, f32[1,512,1,8,64]{1,0,4,3,2:T(1,128)S(1)} %copy.99, s32[]{:T(128)} %get-tuple-element.550, s32[]{:T(128)} %constant.54.clone.1..sunk.1, s32[]{:T(128)} %constant.54.clone.1..sunk.1, s32[]{:T(128)} %constant.54.clone.1..sunk.1, s32[]{:T(128)} %constant.54.clone.1..sunk.1) | dynamic-update-slice | bytes 2097156 | tf_op jit(solution)/shard_map/while/body/jit(dynamic_update_index_in_dim)/dynamic_update_slice | solution.py:242
  963.4 5.1 fusion.183
  968.6 7.6 fusion.184
  979.0 3.2 reshape.481
  988.4 3.3 fusion.65
  992.4 4.6 fusion.72
  997.0 6.9 fusion.107
  1005.1 7.8 fusion.78
  1013.0 269.4 %all-reduce.9.cloned.1.call-done = (bf16[1024,2048]{1,0:T(8,128)(2,1)}, bf16[1024,2048]{1,0:T(8,128)(2,1)}) async-done(((bf16[1024,2048]{1,0:T(8,128)(2,1)}, bf16[1024,2048]{1,0:T(8,128)(2,1)}), (bf16[1024,2048]{1,0:T(8,128)(2,1)}, bf16[1024,2048]{1,0:T(8,128)(2,1)})) %all-reduce.9.cloned.1.call-update) | async-done | bytes 8388624 | tf_op jit(solution)/shard_map/psum | solution.py:177
  1282.4 5.0 fusion.63
  1288.9 11.3 fusion.124
  1300.9 21.0 %convolution_bitcast_fusion.2 = f32[2,2048,1408]{1,2,0:T(8,128)} fusion(bf16[1,1024,1408]{2,1,0:T(8,128)(2,1)} %copy-done.57, bf16[1,1024,1408]{2,1,0:T(8,128)(2,1)} %copy-done.56, f32[1024,2048]{1,0:T(8,128)} %get-tuple-element.339, f32[2048]{0:T(1024)S(1)} %bitcast.367, f32[1024]{0:T(1024)S(1)} %copy-done.47), kind=kOutput, calls=%fused_computation.61 | convolution fusion | flops 11820335104 | bytes 37236736 | tf_op jit(solution)/shard_map/nd,snf->sdf/dot_general | solution.py:200
  1321.9 3.4 copy.71
  1326.0 3.4 copy.68
  1329.4 3.5 copy.69
  1334.4 41.6 %reduce-scatter.9.cloned.1.call-done = f32[256,512]{1,0:T(8,128)} async-done(((f32[2048,512]{1,0:T(8,128)}), f32[256,512]{1,0:T(8,128)}) %reduce-scatter.9.cloned.1.call-update) | async-done | bytes 524304 | tf_op jit(solution)/shard_map/reduce_scatter | solution.py:268
  1379.0 51.8 %reduce-scatter.13.cloned.1.call-done = f32[512,256]{1,0:T(8,128)} async-done(((f32[512,2048]{1,0:T(8,128)}), f32[512,256]{1,0:T(8,128)}) %reduce-scatter.13.cloned.1.call-update) | async-done | bytes 524304 | tf_op jit(solution)/shard_map/reduce_scatter | solution.py:270
  1433.3 37.4 %reduce-scatter.19.cloned.1.call-done = f32[256,2]{1,0:T(8,128)} async-done(((f32[2048,2]{1,0:T(8,128)}), f32[256,2]{1,0:T(8,128)}) %reduce-scatter.19.cloned.1.call-update) | async-done | bytes 2064
  1472.9 87.9 %reduce-scatter.17.cloned.1.call-done = f32[1408,256]{1,0:T(8,128)} async-done(((f32[1408,2048]{1,0:T(8,128)}), f32[1408,256]{1,0:T(8,128)}) %reduce-scatter.17.cloned.1.call-update) | async-done | bytes 1441808 | tf_op jit(solution)/shard_map/reduce_scatter | solution.py:272
  1563.2 147.2 %reduce-scatter.15.cloned.1.call-done = f32[2,256,1408]{1,2,0:T(8,128)} async-done(((f32[2,2048,1408]{1,2,0:T(8,128)}), f32[2,256,1408]{1,2,0:T(8,128)}) %reduce-scatter.15.cloned.1.call-update) | async-done | bytes 2883600 | tf_op jit(solution)/shard_map/reduce_scatter | solution.py:271
  1714.9 9.5 fusion.60
  1724.3 12.2 psum.46
  1736.5 8.3 add_convert_fusion
  1744.8 12.7 psum.47
  1758.2 7.7 multiply_subtract_fusion
  1765.9 3.4 copy.72
  1769.2 3.4 copy.73
  1772.6 3.5 copy.74
  1776.8 5.1 multiply_subtract_fusion.1
  (245 shorter events, 67.7 us)
Async XLA Ops:
  7.2 18.8 %copy-start.33 = (f32[2,256,64]{1,2,0:T(8,128)S(1)}, f32[2,256,64]{1,2,0:T(8,128)}, u32[]{:S(2)}) copy-start(f32[2,256,64]{1,2,0:T(8,128)} %param.36) | copy-start | bytes 393220
  7.2 37.8 %all-gather.5.cloned.1.call-start = ((), (), s32[]{:S(2)}) async-start(), calls=%async_computation.6 | async-start | bytes 2359296 | tf_op jit(solution)/shard_map/all_gather | solution.py:104
  9.1 77.9 %all-gather.7.cloned.1.call-start = ((), (), s32[]{:S(2)}) async-start(), calls=%async_computation.7 | async-start | bytes 2359296 | tf_op jit(solution)/shard_map/all_gather | solution.py:106
  10.9 375.3 %all-reduce.5.cloned.1.call-start = ((), (), s32[]{:S(2)}) async-start(), calls=%async_computation.8 | async-start | bytes 16777216 | tf_op jit(solution)/shard_map/psum | solution.py:168
  11.0 29.2 %copy-start.2 = (bf16[1024,2048]{1,0:T(8,128)(2,1)S(1)}, bf16[1024,2048]{1,0:T(8,128)(2,1)}, u32[]{:S(2)}) copy-start(bf16[1024,2048]{1,0:T(8,128)(2,1)} %param.26) | copy-start | bytes 12582916
  22.9 22.1 %copy-start.42 = (f32[1,2048]{1,0:T(1,128)}, f32[1,2048]{1,0:T(1,128)S(1)}, u32[]{:S(2)}) copy-start(f32[1,2048]{1,0:T(1,128)S(1)} %get-tuple-element.356) | copy-start | bytes 24580
  26.0 19.0 %copy-start.48 = (f32[1024]{0:T(1024)}, f32[1024]{0:T(1024)S(1)}, u32[]{:S(2)}) copy-start(f32[1024]{0:T(1024)S(1)} %add_rsqrt_fusion.1) | copy-start | bytes 12292
  44.3 6.1 copy-start.29
  44.4 6.2 copy-start.17
  44.4 6.2 copy-start.19
  87.0 7.8 copy-start.15
  87.0 7.8 copy-start.31
  94.8 3.3 copy-start.13
  94.8 360.5 %all-gather.9.cloned.1.call-start = ((), (), s32[]{:S(2)}) async-start(), calls=%async_computation.9 | async-start | bytes 12976128 | tf_op jit(solution)/shard_map/all_gather | solution.py:107
  98.0 404.0 %all-gather.11.cloned.1.call-start = ((), (), s32[]{:S(2)}) async-start(), calls=%async_computation.10 | async-start | bytes 6488064 | tf_op jit(solution)/shard_map/all_gather | solution.py:108
  99.0 356.3 %copy-start.44 = (f32[1,2048]{1,0:T(1,128)S(1)}, f32[1,2048]{1,0:T(1,128)}, u32[]{:S(2)}) copy-start(f32[1,2048]{1,0:T(1,128)} %get-tuple-element.355) | copy-start | bytes 24580
  99.1 729.1 %all-reduce.7.cloned.1.call-start = ((), (), s32[]{:S(2)}) async-start(), calls=%async_computation.11 | async-start | bytes 16777216 | tf_op jit(solution)/shard_map/psum | solution.py:206
  395.5 440.3 %copy-start.46 = (f32[1024]{0:T(1024)}, f32[1024]{0:T(1024)S(1)}, u32[]{:S(2)}) copy-start(f32[1024]{0:T(1024)S(1)} %add_rsqrt_fusion) | copy-start | bytes 12292
  517.6 2.5 copy-start.57
  537.2 745.2 %all-reduce.9.cloned.1.call-start = ((), (), s32[]{:S(2)}) async-start(), calls=%async_computation.18 | async-start | bytes 16777216 | tf_op jit(solution)/shard_map/psum | solution.py:177
  828.2 8.2 copy-start.5
  828.2 9.4 copy-start.16
  837.6 4.7 copy-start.55
  842.3 3.7 copy-start.1
  846.1 4.6 copy-start.3
  873.7 3.7 copy-start
  877.4 20.6 %copy-start.7 = (f32[1024,1,64]{0,2,1:T(8,128)S(1)}, f32[1024,1,64]{0,2,1:T(8,128)}, u32[]{:S(2)}) copy-start(f32[1024,1,64]{0,2,1:T(8,128)} %get-tuple-element.551) | copy-start | bytes 786436 | tf_op jit(solution)/shard_map/while
  898.0 5.2 copy-start.6
  898.0 5.2 copy-start.10
  903.2 7.6 copy-start.8
  903.2 8.3 copy-start.4
  911.5 4.6 copy-start.3
  939.0 3.7 copy-start
  942.8 20.6 %copy-start.7 = (f32[1024,1,64]{0,2,1:T(8,128)S(1)}, f32[1024,1,64]{0,2,1:T(8,128)}, u32[]{:S(2)}) copy-start(f32[1024,1,64]{0,2,1:T(8,128)} %get-tuple-element.551) | copy-start | bytes 786436 | tf_op jit(solution)/shard_map/while
  963.4 5.2 copy-start.6
  963.4 5.2 copy-start.10
  968.5 7.6 copy-start.8
  968.6 8.3 copy-start.4
  976.9 5.4 copy-start.18
  982.5 1.8 copy-start.9
  986.0 2.4 copy-start.22
  991.7 341.1 %reduce-scatter.11.cloned.1.call-start = ((), (), s32[]{:S(2)}) async-start(), calls=%async_computation.13 | async-start | bytes 1179648 | tf_op jit(solution)/shard_map/reduce_scatter | solution.py:269
  997.0 379.0 %reduce-scatter.9.cloned.1.call-start = ((), (), s32[]{:S(2)}) async-start(), calls=%async_computation.12 | async-start | bytes 4718592 | tf_op jit(solution)/shard_map/reduce_scatter | solution.py:268
  1003.9 426.9 %reduce-scatter.13.cloned.1.call-start = ((), (), s32[]{:S(2)}) async-start(), calls=%async_computation.14 | async-start | bytes 4718592 | tf_op jit(solution)/shard_map/reduce_scatter | solution.py:270
  1013.0 457.7 %reduce-scatter.19.cloned.1.call-start = ((), (), s32[]{:S(2)}) async-start(), calls=%async_computation.17 | async-start | bytes 1179648
  1282.4 5.0 copy-start.50
  1288.8 272.0 %reduce-scatter.17.cloned.1.call-start = ((), (), s32[]{:S(2)}) async-start(), calls=%async_computation.16 | async-start | bytes 12976128 | tf_op jit(solution)/shard_map/reduce_scatter | solution.py:272
  1300.2 410.2 %reduce-scatter.15.cloned.1.call-start = ((), (), s32[]{:S(2)}) async-start(), calls=%async_computation.15 | async-start | bytes 25952256 | tf_op jit(solution)/shard_map/reduce_scatter | solution.py:271
  1772.6 3.5 copy-start.51
  1772.6 3.5 copy-start.52
  1772.6 3.5 copy-start.53
  1772.6 4.1 copy-start.14
  1776.8 5.2 copy-start.23
  1776.8 5.2 copy-start.26
  1776.8 5.2 copy-start.36
  1776.8 5.2 copy-start.37
  1776.8 6.6 copy-start.34
  1776.8 6.6 copy-start.35
  1776.8 6.6 copy-start.40
  1776.8 6.6 copy-start.41
  1782.0 2.3 copy-start.24
  1782.0 2.2 copy-start.25
  1782.0 2.2 copy-start.38
  1782.0 2.2 copy-start.39
  (15 other events, 17.0 us)
Sparse Core Ops, SparseCore 0:
  10.5 32.9 all-gather.4
  45.9 28.5 all-gather.6
  94.9 291.2 all-reduce.4
  388.6 66.6 all-gather.8
  457.6 44.3 all-gather.10
  537.3 290.8 all-reduce.6
  991.8 290.5 all-reduce.8
  1286.2 35.0 reduce-scatter.10
  1324.6 51.3 reduce-scatter.8
  1379.5 51.2 reduce-scatter.12
  1434.6 36.0 reduce-scatter.18
  1474.0 86.7 reduce-scatter.16
  1564.4 145.9 reduce-scatter.14
